TPU v7x, 32 devices: a whole 2x2x4 slice. The times are simulated.
32 devices in a mesh: along: 2 (over core), across: 4 (over y, x), chan: 4 (over z).
Axes of the slice: x: 2, y: 2, z: 4, core: 2. Of those that a mesh axis runs over, the one named last changes fastest.
Arguments:
- jacobian: float32 [8, 32, 512, 384], P('along', 'across', 'chan'), may hold values from -0.3125 to 0.3125
- departures: float32 [8, 32, 512], P('along', 'across', 'chan'), may hold values from -6 to 6
- inv_variance: float32 [512], P('chan'), may hold values from 0.3 to 3
- channel_use: int32 [512], P('chan'), may hold values 0 or 1
- clear_flags: int32 [8, 32], P('along', 'across'), may hold values 0 or 1
- coefficients: float32 [25, 384], replicated, may hold values from -1.25 to 1.25
Outputs:
- control: float32 [8, 32, 384], P('along', 'across')
- increment: float32 [8, 32, 384], P('along', 'across')
- residual: float32 [8, 32, 384], P('along', 'across')
All inputs are finite; a program needn't handle non-finite values. No bound on the sum of `channel_use` or of `clear_flags` on one device may be relied on, other than what follows from the above.
Results may differ from a plain program's by a relative error of at most 0.0003.
Values sent between devices are 32-bit elements; how exact they have to be, the bound alone decides.
A program may use at most 64 MiB of HBM per device.

v0:
```python
import jax
import jax.numpy as jnp
from jax import lax
from jax.sharding import PartitionSpec as P

ITERS = 10


def extended(cells, sides, width):
    for axis, dim in sides:
        count = lax.axis_size(axis)
        ends = count - 1
        head = lax.slice_in_dim(cells, 0, width, axis=dim)
        tail = lax.slice_in_dim(cells, cells.shape[dim] - width, cells.shape[dim], axis=dim)
        cells = jnp.concatenate(
            [
                lax.ppermute(tail, axis, [(i, (i + 1) % count) for i in range(ends)]),
                cells,
                lax.ppermute(head, axis, [((i + 1) % count, i) for i in range(ends)]),
            ],
            axis=dim,
        )
    return cells


def widen_rim(field):
    return extended(field, (("along", 0), ("across", 1)), 2)


def spread(field, local_coef):
    rows_here, cols_here = (field.shape[0], field.shape[1])
    padded = widen_rim(field)
    result = jnp.zeros(field.shape, jnp.float32)
    for row_shift in range(5):
        for col_shift in range(5):
            result = (
                result
                + local_coef[row_shift * 5 + col_shift]
                * padded[row_shift : row_shift + rows_here, col_shift : col_shift + cols_here]
            )
    return result


def spread_back(field, local_coef):
    rows_here, cols_here = (field.shape[0], field.shape[1])
    padded = widen_rim(field)
    result = jnp.zeros(field.shape, jnp.float32)
    for row_shift in range(5):
        for col_shift in range(5):
            result = (
                result
                + local_coef[row_shift * 5 + col_shift]
                * padded[
                    4 - row_shift : 4 - row_shift + rows_here,
                    4 - col_shift : 4 - col_shift + cols_here,
                ]
            )
    return result


def on_device(jacobian, departures, inv_variance, channel_use, clear_flags, coefficients):
    weight = (
        inv_variance[None, None, :]
        * channel_use.astype(jnp.float32)[None, None, :]
        * clear_flags.astype(jnp.float32)[:, :, None]
    )

    def forward(field):
        return jnp.einsum("xycs,xys->xyc", jacobian, field, precision=lax.Precision.HIGHEST)

    def back_project(weighted):
        adjoint_obs = jnp.einsum(
            "xycs,xyc->xys", jacobian, weighted, precision=lax.Precision.HIGHEST
        )
        return lax.psum(adjoint_obs, "chan")

    def hessian(direction):
        return direction + spread_back(
            back_project(weight * forward(spread(direction, coefficients))), coefficients
        )

    def inner_pair(first, second, third, fourth):
        return lax.psum((jnp.sum(first * second), jnp.sum(third * fourth)), ("along", "across"))

    rhs = spread_back(back_project(weight * departures), coefficients)
    control = jnp.zeros_like(rhs)
    image = hessian(rhs)
    norm_now, product = inner_pair(rhs, rhs, rhs, image)
    alpha = norm_now / product

    def cg_step(step_index, state_tuple):
        control, residual, direction, conj_image, norm_now, alpha = state_tuple
        control = control + alpha * direction
        residual = residual - alpha * conj_image
        image = hessian(residual)
        fresh_norm, product = inner_pair(residual, residual, residual, image)
        beta_ratio = fresh_norm / norm_now
        alpha_next = fresh_norm / (product - beta_ratio * fresh_norm / alpha)
        direction = residual + beta_ratio * direction
        conj_image = image + beta_ratio * conj_image
        return (control, residual, direction, conj_image, fresh_norm, alpha_next)

    control, residual, direction, conj_image, norm_now, alpha = lax.fori_loop(
        0, ITERS - 1, cg_step, (control, rhs, rhs, image, norm_now, alpha)
    )
    control = control + alpha * direction
    residual = residual - alpha * conj_image
    increment = spread(control, coefficients)
    return (control, increment, residual)


def solution(mesh):
    return jax.shard_map(
        on_device,
        mesh=mesh,
        in_specs=(
            P("along", "across", "chan", None),
            P("along", "across", "chan"),
            P("chan"),
            P("chan"),
            P("along", "across"),
            P(),
        ),
        out_specs=(
            P("along", "across", None),
            P("along", "across", None),
            P("along", "across", None),
        ),
        check_vma=False,
    )
```

profile of v0, /device:TPU:0, one launch (start us, length us, event | category | flops | bytes accessed | tf_op | source)
XLA Modules:
  0.0 830.2 jit_solution(16266260684753608233)
XLA Ops:
  8.6 21.3 %psum.49 = f32[4,8,384]{2,1,0:T(8,128)S(1)} all-reduce(f32[4,8,384]{2,1,0:T(8,128)S(1)} %bitcast.53), channel_id=1, replica_groups=mesh['along'=2,'across'=4,'chan'=4] {'chan'}, use_global_device_ids=true, to_apply=%region_0.0 | all-reduce | flops 12288 | bytes 98304 | tf_op jit(solution)/shard_map/psum | solution.py:75
  57.9 8.7 %fusion.284 = f32[4,8,1,128]{3,2,1,0:T(1,128)S(1)} fusion(f32[4,8,128,384]{3,2,1,0:T(8,128)} %param.8, f32[4,8,384,1]{2,1,0,3:T(8,128)S(1)} %fusion.135), kind=kOutput, calls=%fused_computation.537 | convolution fusion | flops 18874368 | bytes 6356992 | tf_op jit(solution)/shard_map/xycs,xys->xyc/dot_general | solution.py:69
  70.4 16.2 %psum.50 = f32[4,8,384]{2,1,0:T(8,128)S(1)} all-reduce(f32[4,8,384]{2,1,0:T(8,128)S(1)} %bitcast.54), channel_id=1, replica_groups=mesh['along'=2,'across'=4,'chan'=4] {'chan'}, use_global_device_ids=true, to_apply=%region_1.0 | all-reduce | flops 12288 | bytes 98304 | tf_op jit(solution)/shard_map/psum | solution.py:75
  99.9 17.4 %all-reduce.1 = (f32[]{:T(128)}, f32[]{:T(128)}) all-reduce(f32[]{:T(128)} %get-tuple-element.132, f32[]{:T(128)} %get-tuple-element.131), channel_id=1, replica_groups=mesh['along'=2,'across'=4,'chan'=4] {'along','across'}, use_global_device_ids=true, to_apply=%region_3.0 | all-reduce | flops 2 | bytes 16 | tf_op jit(solution)/shard_map/psum | solution.py:83
  118.6 697.0 %while.21 = (s32[]{:T(128)}, f32[4,8,384]{2,1,0:T(8,128)S(1)}, f32[4,8,384]{2,1,0:T(8,128)S(1)}, f32[4,8,384]{2,1,0:T(8,128)S(1)}, f32[4,8,384]{2,1,0:T(8,128)S(...) while((s32[]{:T(128)}, f32[4,8,384]{2,1,0:T(8,128)S(1)}, ...), condition=%wide.region_12.0_spmd.clone, body=%wide.region_6.0_spmd.clone.sunk | while | flops 39649280 | bytes 42392784 | solution.py:103
  146.7 17.9 %psum.57 = f32[4,8,384]{2,1,0:T(8,128)S(1)} all-reduce(f32[4,8,384]{2,1,0:T(8,128)S(1)} %bitcast.50), channel_id=1, replica_groups=mesh['along'=2,'across'=4,'chan'=4] {'chan'}, use_global_device_ids=true, to_apply=%region_9.0 | all-reduce | flops 12288 | bytes 98304 | tf_op jit(solution)/shard_map/while/body/eval_jaxpr/psum | solution.py:75
  179.3 15.4 %all-reduce.3 = (f32[]{:T(128)}, f32[]{:T(128)}) all-reduce(f32[]{:T(128)} %get-tuple-element.399, f32[]{:T(128)} %get-tuple-element.400), channel_id=1, replica_groups=mesh['along'=2,'across'=4,'chan'=4] {'along','across'}, use_global_device_ids=true, to_apply=%region_8.0 | all-reduce | flops 2 | bytes 16 | tf_op jit(solution)/shard_map/while/body/eval_jaxpr/psum | solution.py:83
  212.4 8.7 %fusion.324 = f32[4,8,1,128]{3,2,1,0:T(1,128)S(1)} fusion(f32[4,8,128,384]{3,2,1,0:T(8,128)} %get-tuple-element.441, f32[4,8,384,1]{2,1,0,3:T(8,128)S(1)} %fusion.323), kind=kOutput, calls=%fused_computation.166.clone.1 | convolution fusion | flops 18874368 | bytes 6356992 | tf_op jit(solution)/shard_map/while/body/eval_jaxpr/xycs,xys->xyc/dot_general | solution.py:69
  224.8 16.5 %psum.57 = f32[4,8,384]{2,1,0:T(8,128)S(1)} all-reduce(f32[4,8,384]{2,1,0:T(8,128)S(1)} %bitcast.50), channel_id=1, replica_groups=mesh['along'=2,'across'=4,'chan'=4] {'chan'}, use_global_device_ids=true, to_apply=%region_9.0 | all-reduce | flops 12288 | bytes 98304 | tf_op jit(solution)/shard_map/while/body/eval_jaxpr/psum | solution.py:75
  256.8 14.3 %all-reduce.3 = (f32[]{:T(128)}, f32[]{:T(128)}) all-reduce(f32[]{:T(128)} %get-tuple-element.399, f32[]{:T(128)} %get-tuple-element.400), channel_id=1, replica_groups=mesh['along'=2,'across'=4,'chan'=4] {'along','across'}, use_global_device_ids=true, to_apply=%region_8.0 | all-reduce | flops 2 | bytes 16 | tf_op jit(solution)/shard_map/while/body/eval_jaxpr/psum | solution.py:83
  301.3 17.8 %psum.57 = f32[4,8,384]{2,1,0:T(8,128)S(1)} all-reduce(f32[4,8,384]{2,1,0:T(8,128)S(1)} %bitcast.50), channel_id=1, replica_groups=mesh['along'=2,'across'=4,'chan'=4] {'chan'}, use_global_device_ids=true, to_apply=%region_9.0 | all-reduce | flops 12288 | bytes 98304 | tf_op jit(solution)/shard_map/while/body/eval_jaxpr/psum | solution.py:75
  334.9 14.3 %all-reduce.3 = (f32[]{:T(128)}, f32[]{:T(128)}) all-reduce(f32[]{:T(128)} %get-tuple-element.399, f32[]{:T(128)} %get-tuple-element.400), channel_id=1, replica_groups=mesh['along'=2,'across'=4,'chan'=4] {'along','across'}, use_global_device_ids=true, to_apply=%region_8.0 | all-reduce | flops 2 | bytes 16 | tf_op jit(solution)/shard_map/while/body/eval_jaxpr/psum | solution.py:83
  379.4 16.5 %psum.57 = f32[4,8,384]{2,1,0:T(8,128)S(1)} all-reduce(f32[4,8,384]{2,1,0:T(8,128)S(1)} %bitcast.50), channel_id=1, replica_groups=mesh['along'=2,'across'=4,'chan'=4] {'chan'}, use_global_device_ids=true, to_apply=%region_9.0 | all-reduce | flops 12288 | bytes 98304 | tf_op jit(solution)/shard_map/while/body/eval_jaxpr/psum | solution.py:75
  411.4 14.3 %all-reduce.3 = (f32[]{:T(128)}, f32[]{:T(128)}) all-reduce(f32[]{:T(128)} %get-tuple-element.399, f32[]{:T(128)} %get-tuple-element.400), channel_id=1, replica_groups=mesh['along'=2,'across'=4,'chan'=4] {'along','across'}, use_global_device_ids=true, to_apply=%region_8.0 | all-reduce | flops 2 | bytes 16 | tf_op jit(solution)/shard_map/while/body/eval_jaxpr/psum | solution.py:83
  455.9 17.8 %psum.57 = f32[4,8,384]{2,1,0:T(8,128)S(1)} all-reduce(f32[4,8,384]{2,1,0:T(8,128)S(1)} %bitcast.50), channel_id=1, replica_groups=mesh['along'=2,'across'=4,'chan'=4] {'chan'}, use_global_device_ids=true, to_apply=%region_9.0 | all-reduce | flops 12288 | bytes 98304 | tf_op jit(solution)/shard_map/while/body/eval_jaxpr/psum | solution.py:75
  489.5 14.3 %all-reduce.3 = (f32[]{:T(128)}, f32[]{:T(128)}) all-reduce(f32[]{:T(128)} %get-tuple-element.399, f32[]{:T(128)} %get-tuple-element.400), channel_id=1, replica_groups=mesh['along'=2,'across'=4,'chan'=4] {'along','across'}, use_global_device_ids=true, to_apply=%region_8.0 | all-reduce | flops 2 | bytes 16 | tf_op jit(solution)/shard_map/while/body/eval_jaxpr/psum | solution.py:83
  534.0 16.5 %psum.57 = f32[4,8,384]{2,1,0:T(8,128)S(1)} all-reduce(f32[4,8,384]{2,1,0:T(8,128)S(1)} %bitcast.50), channel_id=1, replica_groups=mesh['along'=2,'across'=4,'chan'=4] {'chan'}, use_global_device_ids=true, to_apply=%region_9.0 | all-reduce | flops 12288 | bytes 98304 | tf_op jit(solution)/shard_map/while/body/eval_jaxpr/psum | solution.py:75
  566.0 14.3 %all-reduce.3 = (f32[]{:T(128)}, f32[]{:T(128)}) all-reduce(f32[]{:T(128)} %get-tuple-element.399, f32[]{:T(128)} %get-tuple-element.400), channel_id=1, replica_groups=mesh['along'=2,'across'=4,'chan'=4] {'along','across'}, use_global_device_ids=true, to_apply=%region_8.0 | all-reduce | flops 2 | bytes 16 | tf_op jit(solution)/shard_map/while/body/eval_jaxpr/psum | solution.py:83
  610.5 17.8 %psum.57 = f32[4,8,384]{2,1,0:T(8,128)S(1)} all-reduce(f32[4,8,384]{2,1,0:T(8,128)S(1)} %bitcast.50), channel_id=1, replica_groups=mesh['along'=2,'across'=4,'chan'=4] {'chan'}, use_global_device_ids=true, to_apply=%region_9.0 | all-reduce | flops 12288 | bytes 98304 | tf_op jit(solution)/shard_map/while/body/eval_jaxpr/psum | solution.py:75
  644.0 14.3 %all-reduce.3 = (f32[]{:T(128)}, f32[]{:T(128)}) all-reduce(f32[]{:T(128)} %get-tuple-element.399, f32[]{:T(128)} %get-tuple-element.400), channel_id=1, replica_groups=mesh['along'=2,'across'=4,'chan'=4] {'along','across'}, use_global_device_ids=true, to_apply=%region_8.0 | all-reduce | flops 2 | bytes 16 | tf_op jit(solution)/shard_map/while/body/eval_jaxpr/psum | solution.py:83
  688.5 16.5 %psum.57 = f32[4,8,384]{2,1,0:T(8,128)S(1)} all-reduce(f32[4,8,384]{2,1,0:T(8,128)S(1)} %bitcast.50), channel_id=1, replica_groups=mesh['along'=2,'across'=4,'chan'=4] {'chan'}, use_global_device_ids=true, to_apply=%region_9.0 | all-reduce | flops 12288 | bytes 98304 | tf_op jit(solution)/shard_map/while/body/eval_jaxpr/psum | solution.py:75
  720.5 14.3 %all-reduce.3 = (f32[]{:T(128)}, f32[]{:T(128)}) all-reduce(f32[]{:T(128)} %get-tuple-element.399, f32[]{:T(128)} %get-tuple-element.400), channel_id=1, replica_groups=mesh['along'=2,'across'=4,'chan'=4] {'along','across'}, use_global_device_ids=true, to_apply=%region_8.0 | all-reduce | flops 2 | bytes 16 | tf_op jit(solution)/shard_map/while/body/eval_jaxpr/psum | solution.py:83
  765.1 17.8 %psum.57 = f32[4,8,384]{2,1,0:T(8,128)S(1)} all-reduce(f32[4,8,384]{2,1,0:T(8,128)S(1)} %bitcast.50), channel_id=1, replica_groups=mesh['along'=2,'across'=4,'chan'=4] {'chan'}, use_global_device_ids=true, to_apply=%region_9.0 | all-reduce | flops 12288 | bytes 98304 | tf_op jit(solution)/shard_map/while/body/eval_jaxpr/psum | solution.py:75
  798.6 14.3 %all-reduce.3 = (f32[]{:T(128)}, f32[]{:T(128)}) all-reduce(f32[]{:T(128)} %get-tuple-element.399, f32[]{:T(128)} %get-tuple-element.400), channel_id=1, replica_groups=mesh['along'=2,'across'=4,'chan'=4] {'along','across'}, use_global_device_ids=true, to_apply=%region_8.0 | all-reduce | flops 2 | bytes 16 | tf_op jit(solution)/shard_map/while/body/eval_jaxpr/psum | solution.py:83
  (398 shorter events, 439.6 us)
Async XLA Ops:
  34.3 5.9 collective-permute-start.10
  35.6 6.1 collective-permute-start.11
  46.3 5.9 collective-permute-start.14
  50.6 7.2 collective-permute-start.15
  91.0 6.7 collective-permute-start.18
  92.3 6.8 collective-permute-start.19
  172.8 5.7 collective-permute-start.7
  205.3 6.9 collective-permute-start.3
  245.7 6.5 collective-permute-start.6
  282.3 6.4 collective-permute-start.3
  323.6 6.8 collective-permute-start.6
  360.3 6.4 collective-permute-start.3
  400.3 6.5 collective-permute-start.6
  436.9 6.4 collective-permute-start.3
  478.1 6.8 collective-permute-start.6
  514.9 6.4 collective-permute-start.3
  554.9 6.5 collective-permute-start.6
  591.4 6.4 collective-permute-start.3
  632.7 6.8 collective-permute-start.6
  669.5 6.4 collective-permute-start.3
  709.4 6.5 collective-permute-start.6
  746.0 6.4 collective-permute-start.3
  787.3 6.8 collective-permute-start.6
  823.0 6.4 collective-permute-start.23
  (77 other events, 596.9 us)
where the time goes:
time: 833 us; the launch traced here: 830 us
  blocking collectives  340 us (41%)
  starting transfers between devices  189 us (23%)
  matrix products  129 us (15%)
  waiting for transfers between devices  122 us (15%)
  loops' own time  31.3 us (4%)
  other arithmetic  14.8 us (2%)
    psum x11, blocking collectives, back_project(): return lax.psum(adjoint_obs, 'chan')  192 us
    psum x10, blocking collectives, inner_pair(): lax.psum((jnp.sum(first * second), jnp.sum(third * fourth)), ('along', 'a...  147 us
    ppermute x44, starting transfers between devices, extended(): lax.ppermute(tail, axis, [(i, (i + 1) % count) for i in range(ends)])  130 us
    ppermute x44, waiting for transfers between devices, extended(): lax.ppermute(head, axis, [((i + 1) % count, i) for i in range(ends)])  111 us
    dot_general x10, matrix products, forward(): jnp.einsum('xycs,xys->xyc', jacobian, field, precision=lax.Precision.HIGH...  87.2 us
    ppermute x44, starting transfers between devices, extended(): lax.ppermute(head, axis, [((i + 1) % count, i) for i in range(ends)])  59.5 us
    dot_general x11, matrix products, back_project(): jnp.einsum('xycs,xyc->xys', jacobian, weighted, precision=lax.Precision.H...  42.1 us
    another operation x1, loops' own time, on_device(): lax.fori_loop(0, ITERS - 1, cg_step, (control, rhs, rhs, image, norm_now,...  31.3 us
  transfers between devices with their start and end apart: 88, of which 53 were waited for; matrix products, arithmetic and copies ran while one was open for 0% of the time, Pallas kernels for 0%

commit v1 on v0

--- a/solution.py
+++ b/solution.py
@@ -4,6 +4,11 @@
 from jax.sharding import PartitionSpec as P
 
 ITERS = 10
+
+
+def add_all(x, name):
+    shards = lax.all_gather(x, name)
+    return jnp.sum(shards, axis=0)
 
 
 def extended(cells, sides, width):
@@ -72,7 +77,7 @@
         adjoint_obs = jnp.einsum(
             "xycs,xyc->xys", jacobian, weighted, precision=lax.Precision.HIGHEST
         )
-        return lax.psum(adjoint_obs, "chan")
+        return add_all(adjoint_obs, "chan")
 
     def hessian(direction):
         return direction + spread_back(

time: 833 us -> 801 us (0.962)
  waiting for transfers between devices: 122 us -> 80.2 us
  starting transfers between devices: 189 us -> 216 us
  blocking collectives: 340 us -> 322 us
    psum x11 -> x0, blocking collectives: 192 us -> none  [back_project(): return lax.psum(adjoint_obs, 'chan')]
    all_gather x0 -> x11, blocking collectives: none -> 152 us  [add_all(): shards = lax.all_gather(x, name)]
    ppermute x44, waiting for transfers between devices: 111 us -> 54.2 us  [extended(): lax.ppermute(head, axis, [((i + 1) % count, i) for i in range(ends)])]
    ppermute x44, starting transfers between devices: 130 us -> 157 us  [extended(): lax.ppermute(tail, axis, [(i, (i + 1) % count) for i in range(ends)])]
    psum x10, blocking collectives: 147 us -> 170 us  [inner_pair(): lax.psum((jnp.sum(first * second), jnp.sum(third * fourth)), ('along', 'a...]
    ppermute x44, waiting for transfers between devices: 10.9 us -> 26 us  [extended(): lax.ppermute(tail, axis, [(i, (i + 1) % count) for i in range(ends)])]
  transfers between devices with their start and end apart: 88 -> 88, of which waited for: 53 -> 54; matrix products, arithmetic and copies ran while one was open for 0% -> 0% of each run, Pallas kernels for 0% -> 0%
where the time goes in v1:
time: 801 us; the launch traced here: 798 us
  blocking collectives  322 us (40%)
  starting transfers between devices  216 us (27%)
  matrix products  129 us (16%)
  waiting for transfers between devices  80.2 us (10%)
  loops' own time  31.1 us (4%)
  other arithmetic  15.2 us (2%)
    psum x10, blocking collectives, inner_pair(): lax.psum((jnp.sum(first * second), jnp.sum(third * fourth)), ('along', 'a...  170 us
    ppermute x44, starting transfers between devices, extended(): lax.ppermute(tail, axis, [(i, (i + 1) % count) for i in range(ends)])  157 us
    all_gather x11, blocking collectives, add_all(): shards = lax.all_gather(x, name)  152 us
    dot_general x10, matrix products, forward(): jnp.einsum('xycs,xys->xyc', jacobian, field, precision=lax.Precision.HIGH...  87.2 us
    ppermute x44, starting transfers between devices, extended(): lax.ppermute(head, axis, [((i + 1) % count, i) for i in range(ends)])  59.2 us
    ppermute x44, waiting for transfers between devices, extended(): lax.ppermute(head, axis, [((i + 1) % count, i) for i in range(ends)])  54.2 us
    dot_general x11, matrix products, back_project(): jnp.einsum('xycs,xyc->xys', jacobian, weighted, precision=lax.Precision.H...  42.1 us
    another operation x1, loops' own time, on_device(): lax.fori_loop(0, ITERS - 1, cg_step, (control, rhs, rhs, image, norm_now,...  31.1 us
  transfers between devices with their start and end apart: 88, of which 54 were waited for; matrix products, arithmetic and copies ran while one was open for 0% of the time, Pallas kernels for 0%

profile of v1, /device:TPU:0, one launch (start us, length us, event | category | flops | bytes accessed | tf_op | source)
XLA Modules:
  0.0 798.2 jit_solution(8011080568190956837)
XLA Ops:
  8.6 15.5 %all-gather.1 = f32[16,8,384]{2,1,0:T(8,128)S(1)} all-gather(f32[4,8,384]{2,1,0:T(8,128)S(1)} %bitcast.61), channel_id=3, replica_groups=mesh['along'=2,'across'=4,'chan'=4] {'chan'}, dimensions={0}, use_global_device_ids=true | all-gather | bytes 245760 | tf_op jit(solution)/shard_map/all_gather | solution.py:10
  52.2 8.7 %fusion.188 = f32[4,8,1,128]{3,2,1,0:T(1,128)S(1)} fusion(f32[4,8,128,384]{3,2,1,0:T(8,128)} %param.8, f32[4,8,384,1]{2,1,0,3:T(8,128)S(1)} %fusion.131), kind=kOutput, calls=%fused_computation.395 | convolution fusion | flops 18874368 | bytes 6356992 | tf_op jit(solution)/shard_map/xycs,xys->xyc/dot_general | solution.py:74
  64.6 13.7 %all-gather.2 = f32[16,8,384]{2,1,0:T(8,128)S(1)} all-gather(f32[4,8,384]{2,1,0:T(8,128)S(1)} %bitcast.62), channel_id=4, replica_groups=mesh['along'=2,'across'=4,'chan'=4] {'chan'}, dimensions={0}, use_global_device_ids=true | all-gather | bytes 245760 | tf_op jit(solution)/shard_map/all_gather | solution.py:10
  91.8 17.4 %all-reduce.1 = (f32[]{:T(128)}, f32[]{:T(128)}) all-reduce(f32[]{:T(128)} %get-tuple-element.132, f32[]{:T(128)} %get-tuple-element.131), channel_id=1, replica_groups=mesh['along'=2,'across'=4,'chan'=4] {'along','across'}, use_global_device_ids=true, to_apply=%region_3.0 | all-reduce | flops 2 | bytes 16 | tf_op jit(solution)/shard_map/psum | solution.py:88
  110.5 672.5 %while.21 = (s32[]{:T(128)}, f32[4,8,384]{2,1,0:T(8,128)S(1)}, f32[4,8,384]{2,1,0:T(8,128)S(1)}, f32[4,8,384]{2,1,0:T(8,128)S(1)}, f32[4,8,384]{2,1,0:T(8,128)S(...) while((s32[]{:T(128)}, f32[4,8,384]{2,1,0:T(8,128)S(1)}, ...), condition=%wide.region_12.0_spmd.clone, body=%wide.region_6.0_spmd.clone.sunk | while | flops 39686144 | bytes 43572444 | solution.py:108
  126.1 8.7 %fusion.224 = f32[4,8,1,128]{3,2,1,0:T(1,128)S(1)} fusion(f32[4,8,128,384]{3,2,1,0:T(8,128)} %get-tuple-element.418, f32[4,8,384,1]{2,1,0,3:T(8,128)S(1)} %fusion.223), kind=kOutput, calls=%fused_computation.120.clone.1 | convolution fusion | flops 18874368 | bytes 6356992 | tf_op jit(solution)/shard_map/while/body/eval_jaxpr/xycs,xys->xyc/dot_general | solution.py:74
  138.6 13.7 %all-gather.5 = f32[16,8,384]{2,1,0:T(8,128)S(1)} all-gather(f32[4,8,384]{2,1,0:T(8,128)S(1)} %bitcast.56), channel_id=2, replica_groups=mesh['along'=2,'across'=4,'chan'=4] {'chan'}, dimensions={0}, use_global_device_ids=true | all-gather | bytes 245760 | tf_op jit(solution)/shard_map/while/body/eval_jaxpr/all_gather | solution.py:10
  165.6 17.0 %all-reduce.3 = (f32[]{:T(128)}, f32[]{:T(128)}) all-reduce(f32[]{:T(128)} %get-tuple-element.374, f32[]{:T(128)} %get-tuple-element.375), channel_id=1, replica_groups=mesh['along'=2,'across'=4,'chan'=4] {'along','across'}, use_global_device_ids=true, to_apply=%region_8.0 | all-reduce | flops 2 | bytes 16 | tf_op jit(solution)/shard_map/while/body/eval_jaxpr/psum | solution.py:88
  213.3 13.6 %all-gather.5 = f32[16,8,384]{2,1,0:T(8,128)S(1)} all-gather(f32[4,8,384]{2,1,0:T(8,128)S(1)} %bitcast.56), channel_id=2, replica_groups=mesh['along'=2,'across'=4,'chan'=4] {'chan'}, dimensions={0}, use_global_device_ids=true | all-gather | bytes 245760 | tf_op jit(solution)/shard_map/while/body/eval_jaxpr/all_gather | solution.py:10
  240.3 17.0 %all-reduce.3 = (f32[]{:T(128)}, f32[]{:T(128)}) all-reduce(f32[]{:T(128)} %get-tuple-element.374, f32[]{:T(128)} %get-tuple-element.375), channel_id=1, replica_groups=mesh['along'=2,'across'=4,'chan'=4] {'along','across'}, use_global_device_ids=true, to_apply=%region_8.0 | all-reduce | flops 2 | bytes 16 | tf_op jit(solution)/shard_map/while/body/eval_jaxpr/psum | solution.py:88
  288.0 13.6 %all-gather.5 = f32[16,8,384]{2,1,0:T(8,128)S(1)} all-gather(f32[4,8,384]{2,1,0:T(8,128)S(1)} %bitcast.56), channel_id=2, replica_groups=mesh['along'=2,'across'=4,'chan'=4] {'chan'}, dimensions={0}, use_global_device_ids=true | all-gather | bytes 245760 | tf_op jit(solution)/shard_map/while/body/eval_jaxpr/all_gather | solution.py:10
  315.1 17.0 %all-reduce.3 = (f32[]{:T(128)}, f32[]{:T(128)}) all-reduce(f32[]{:T(128)} %get-tuple-element.374, f32[]{:T(128)} %get-tuple-element.375), channel_id=1, replica_groups=mesh['along'=2,'across'=4,'chan'=4] {'along','across'}, use_global_device_ids=true, to_apply=%region_8.0 | all-reduce | flops 2 | bytes 16 | tf_op jit(solution)/shard_map/while/body/eval_jaxpr/psum | solution.py:88
  362.8 13.6 %all-gather.5 = f32[16,8,384]{2,1,0:T(8,128)S(1)} all-gather(f32[4,8,384]{2,1,0:T(8,128)S(1)} %bitcast.56), channel_id=2, replica_groups=mesh['along'=2,'across'=4,'chan'=4] {'chan'}, dimensions={0}, use_global_device_ids=true | all-gather | bytes 245760 | tf_op jit(solution)/shard_map/while/body/eval_jaxpr/all_gather | solution.py:10
  389.8 17.0 %all-reduce.3 = (f32[]{:T(128)}, f32[]{:T(128)}) all-reduce(f32[]{:T(128)} %get-tuple-element.374, f32[]{:T(128)} %get-tuple-element.375), channel_id=1, replica_groups=mesh['along'=2,'across'=4,'chan'=4] {'along','across'}, use_global_device_ids=true, to_apply=%region_8.0 | all-reduce | flops 2 | bytes 16 | tf_op jit(solution)/shard_map/while/body/eval_jaxpr/psum | solution.py:88
  437.5 13.6 %all-gather.5 = f32[16,8,384]{2,1,0:T(8,128)S(1)} all-gather(f32[4,8,384]{2,1,0:T(8,128)S(1)} %bitcast.56), channel_id=2, replica_groups=mesh['along'=2,'across'=4,'chan'=4] {'chan'}, dimensions={0}, use_global_device_ids=true | all-gather | bytes 245760 | tf_op jit(solution)/shard_map/while/body/eval_jaxpr/all_gather | solution.py:10
  464.5 17.0 %all-reduce.3 = (f32[]{:T(128)}, f32[]{:T(128)}) all-reduce(f32[]{:T(128)} %get-tuple-element.374, f32[]{:T(128)} %get-tuple-element.375), channel_id=1, replica_groups=mesh['along'=2,'across'=4,'chan'=4] {'along','across'}, use_global_device_ids=true, to_apply=%region_8.0 | all-reduce | flops 2 | bytes 16 | tf_op jit(solution)/shard_map/while/body/eval_jaxpr/psum | solution.py:88
  512.2 13.6 %all-gather.5 = f32[16,8,384]{2,1,0:T(8,128)S(1)} all-gather(f32[4,8,384]{2,1,0:T(8,128)S(1)} %bitcast.56), channel_id=2, replica_groups=mesh['along'=2,'across'=4,'chan'=4] {'chan'}, dimensions={0}, use_global_device_ids=true | all-gather | bytes 245760 | tf_op jit(solution)/shard_map/while/body/eval_jaxpr/all_gather | solution.py:10
  539.2 17.0 %all-reduce.3 = (f32[]{:T(128)}, f32[]{:T(128)}) all-reduce(f32[]{:T(128)} %get-tuple-element.374, f32[]{:T(128)} %get-tuple-element.375), channel_id=1, replica_groups=mesh['along'=2,'across'=4,'chan'=4] {'along','across'}, use_global_device_ids=true, to_apply=%region_8.0 | all-reduce | flops 2 | bytes 16 | tf_op jit(solution)/shard_map/while/body/eval_jaxpr/psum | solution.py:88
  586.9 13.6 %all-gather.5 = f32[16,8,384]{2,1,0:T(8,128)S(1)} all-gather(f32[4,8,384]{2,1,0:T(8,128)S(1)} %bitcast.56), channel_id=2, replica_groups=mesh['along'=2,'across'=4,'chan'=4] {'chan'}, dimensions={0}, use_global_device_ids=true | all-gather | bytes 245760 | tf_op jit(solution)/shard_map/while/body/eval_jaxpr/all_gather | solution.py:10
  613.9 17.0 %all-reduce.3 = (f32[]{:T(128)}, f32[]{:T(128)}) all-reduce(f32[]{:T(128)} %get-tuple-element.374, f32[]{:T(128)} %get-tuple-element.375), channel_id=1, replica_groups=mesh['along'=2,'across'=4,'chan'=4] {'along','across'}, use_global_device_ids=true, to_apply=%region_8.0 | all-reduce | flops 2 | bytes 16 | tf_op jit(solution)/shard_map/while/body/eval_jaxpr/psum | solution.py:88
  661.6 13.6 %all-gather.5 = f32[16,8,384]{2,1,0:T(8,128)S(1)} all-gather(f32[4,8,384]{2,1,0:T(8,128)S(1)} %bitcast.56), channel_id=2, replica_groups=mesh['along'=2,'across'=4,'chan'=4] {'chan'}, dimensions={0}, use_global_device_ids=true | all-gather | bytes 245760 | tf_op jit(solution)/shard_map/while/body/eval_jaxpr/all_gather | solution.py:10
  688.6 17.0 %all-reduce.3 = (f32[]{:T(128)}, f32[]{:T(128)}) all-reduce(f32[]{:T(128)} %get-tuple-element.374, f32[]{:T(128)} %get-tuple-element.375), channel_id=1, replica_groups=mesh['along'=2,'across'=4,'chan'=4] {'along','across'}, use_global_device_ids=true, to_apply=%region_8.0 | all-reduce | flops 2 | bytes 16 | tf_op jit(solution)/shard_map/while/body/eval_jaxpr/psum | solution.py:88
  736.3 13.6 %all-gather.5 = f32[16,8,384]{2,1,0:T(8,128)S(1)} all-gather(f32[4,8,384]{2,1,0:T(8,128)S(1)} %bitcast.56), channel_id=2, replica_groups=mesh['along'=2,'across'=4,'chan'=4] {'chan'}, dimensions={0}, use_global_device_ids=true | all-gather | bytes 245760 | tf_op jit(solution)/shard_map/while/body/eval_jaxpr/all_gather | solution.py:10
  763.3 17.0 %all-reduce.3 = (f32[]{:T(128)}, f32[]{:T(128)}) all-reduce(f32[]{:T(128)} %get-tuple-element.374, f32[]{:T(128)} %get-tuple-element.375), channel_id=1, replica_groups=mesh['along'=2,'across'=4,'chan'=4] {'along','across'}, use_global_device_ids=true, to_apply=%region_8.0 | all-reduce | flops 2 | bytes 16 | tf_op jit(solution)/shard_map/while/body/eval_jaxpr/psum | solution.py:88
  (387 shorter events, 425.3 us)
Async XLA Ops:
  28.5 5.9 collective-permute-start.10
  29.8 6.1 collective-permute-start.11
  40.8 5.8 collective-permute-start.14
  45.1 6.9 collective-permute-start.15
  82.7 6.8 collective-permute-start.18
  84.0 7.0 collective-permute-start.19
  157.5 6.5 collective-permute-start.6
  158.8 6.1 collective-permute-start.7
  232.2 6.5 collective-permute-start.6
  233.5 6.1 collective-permute-start.7
  306.9 6.5 collective-permute-start.6
  308.2 6.1 collective-permute-start.7
  381.6 6.5 collective-permute-start.6
  382.9 6.1 collective-permute-start.7
  456.3 6.5 collective-permute-start.6
  457.6 6.1 collective-permute-start.7
  531.0 6.5 collective-permute-start.6
  532.3 6.1 collective-permute-start.7
  605.7 6.5 collective-permute-start.6
  607.0 6.1 collective-permute-start.7
  680.5 6.5 collective-permute-start.6
  681.8 6.1 collective-permute-start.7
  755.2 6.5 collective-permute-start.6
  756.5 6.1 collective-permute-start.7
  (77 other events, 632.7 us)
